TPU v7x, 32 devices: a whole 2x2x4 slice. The times are simulated.
32 devices in a mesh: cube: 8 (over z, y), blk: 4 (over x, core).
Axes of the slice: x: 2, y: 2, z: 4, core: 2. Of those that a mesh axis runs over, the one named last changes fastest.
Arguments:
- rhs_root: bfloat16 [1, 10240, 128], P(None, 'blk'), may hold values from -6 to 6
- rhs_mid: bfloat16 [2, 10240, 128], P(None, 'blk'), may hold values from -6 to 6
- rhs_leaf: bfloat16 [4, 10240, 128], P(None, 'blk'), may hold values from -6 to 6
- pivot_root: bfloat16 [2, 10240, 10240], P(None, 'cube', 'blk'), may hold values from -0.0625 to 0.0625
- pivot_mid: bfloat16 [2, 20480, 10240], P(None, 'cube', 'blk'), may hold values from -0.0625 to 0.0625
- pivot_leaf: bfloat16 [2, 40960, 10240], P(None, 'cube', 'blk'), may hold values from -0.0625 to 0.0625
- coupling_mid: bfloat16 [2, 2560, 10240], P(None, 'cube', 'blk'), may hold values from -0.0625 to 0.0625
- coupling_leaf: bfloat16 [2, 5120, 10240], P(None, 'cube', 'blk'), may hold values from -0.0625 to 0.0625
- front_blocks: int32 [7], replicated, may hold values from 40 to 80, as said below
- child_map: int32 [6, 10], replicated, may hold values from 0 to 79
Outputs:
- solution_root: bfloat16 [4, 2560, 128], P('blk', 'cube')
- solution_mid: bfloat16 [4, 5120, 128], P('blk', 'cube')
- solution_leaf: bfloat16 [4, 10240, 128], P('blk', 'cube')
Inputs may be any that keep to these rules, and one draw needn't show every extreme that they name: `front_blocks`: entry 0 is the root, entries 1 and 2 the level-1 fronts, 3 to 6 the level-2 fronts; at least one front is full in every draw. `child_map`: rows 0 and 1 belong to the level-1 fronts, row 2 + q to level-2 front q; targets may repeat within and across children.
All inputs are finite; a program needn't handle non-finite values.
Results may differ from a plain program's by a relative error of at most 0.013.
Values may be sent and summed in bfloat16 or wider, within the bound.
A program may use at most 192 MiB of HBM per device.

v0:
```python
import jax
import jax.numpy as jnp
from jax import lax
from jax.sharding import PartitionSpec as P

SEPARATOR = 10240
BLOCK_ROWS = 128


def swapped(value, axis, distance):
    return lax.ppermute(value, axis, [(i, i ^ 1 << distance) for i in range(lax.axis_size(axis))])


def rotate_parts(vec):
    half = vec.shape[1] // 2
    return jnp.concatenate([-vec[:, half:], vec[:, :half]], axis=1)


def complex_apply(matrix, vec):
    first = jnp.dot(matrix[0], vec, preferred_element_type=jnp.float32)
    second = jnp.dot(matrix[1], rotate_parts(vec), preferred_element_type=jnp.float32)
    return first + second


def complex_apply_t(matrix, vec):
    dims = (((0,), (0,)), ((), ()))
    first = lax.dot_general(matrix[0], vec, dims, preferred_element_type=jnp.float32)
    second = lax.dot_general(matrix[1], rotate_parts(vec), dims, preferred_element_type=jnp.float32)
    return first + second


def bit_set(cube_at, bit):
    return cube_at >> bit & 1 == 1


def gather_bits(piece, count, cube_at):
    for bit in range(count):
        other = swapped(piece, "cube", bit)
        upper = bit_set(cube_at, bit)
        piece = jnp.where(
            upper, jnp.concatenate([other, piece], 0), jnp.concatenate([piece, other], 0)
        )
    return piece


def swap_sum(value, bit):
    return swapped(value.astype(jnp.bfloat16), "cube", bit).astype(value.dtype)


def halve_bits(total, count, cube_at):
    for bit in reversed(range(count)):
        rows = total.shape[0] // 2
        lower = total[:rows]
        higher = total[rows:]
        upper = bit_set(cube_at, bit)
        sent = jnp.where(upper, lower, higher)
        kept = jnp.where(upper, higher, lower)
        total = kept + swap_sum(sent, bit)
    return total


def blk_total(value):
    return lax.psum(value, "blk")


def row_mask(start, count, limit):
    rows = start + jnp.arange(count, dtype=jnp.int32)
    return (rows < limit).astype(jnp.float32)[:, None]


def extend_add(gathered, targets, first_block, slice_blocks):
    blocks = gathered.reshape(targets.shape[0], BLOCK_ROWS, gathered.shape[1])
    slots = jnp.arange(slice_blocks, dtype=jnp.int32)
    placing = (targets[None, :] - first_block == slots[:, None]).astype(jnp.bfloat16)
    summed = jnp.einsum("ti,ird->trd", placing, blocks, preferred_element_type=jnp.float32)
    return summed.reshape(slice_blocks * BLOCK_ROWS, gathered.shape[1])


def pick_rows(parent_slice, targets, rows, first_row):
    block_of = rows // BLOCK_ROWS
    table = (block_of[:, None] == jnp.arange(targets.shape[0], dtype=jnp.int32)[None, :]).astype(
        jnp.int32
    )
    target_block = jnp.sum(table * targets[None, :], axis=1)
    where_row = target_block * BLOCK_ROWS + rows % BLOCK_ROWS - first_row
    inside = (where_row >= 0) & (where_row < parent_slice.shape[0])
    values = parent_slice[jnp.clip(where_row, 0, parent_slice.shape[0] - 1)].astype(jnp.float32)
    return jnp.where(inside[:, None], values, 0.0)


def forward_front(pivot, coupling, gathered, column_mask, solved_mask):
    masked = (column_mask * gathered).astype(jnp.bfloat16)
    own_rows = pivot.shape[1]
    if coupling is None:
        sums = blk_total(complex_apply(pivot, masked))
        return ((solved_mask * sums).astype(jnp.bfloat16), None)
    both = jnp.concatenate([complex_apply(pivot, masked), complex_apply(coupling, masked)], 0)
    sums = blk_total(both)
    solved = (solved_mask * sums[:own_rows]).astype(jnp.bfloat16)
    return (solved, sums[own_rows:].astype(jnp.bfloat16))


def per_device(
    rhs_root,
    rhs_mid,
    rhs_leaf,
    pivot_root,
    pivot_mid,
    pivot_leaf,
    coupling_mid,
    coupling_leaf,
    front_blocks,
    child_map,
):
    cube_n = lax.axis_size("cube")
    blk_n = lax.axis_size("blk")
    cube_at = lax.axis_index("cube")
    blk_at = lax.axis_index("blk")
    slice_rows = SEPARATOR // blk_n
    slice_blocks = slice_rows // BLOCK_ROWS
    first_row = blk_at * slice_rows
    first_block = blk_at * slice_blocks
    group_mid = cube_n // 2
    group_leaf = cube_n // 4
    bits_root = cube_n.bit_length() - 1
    bits_mid = bits_root - 1
    bits_leaf = bits_root - 2
    front_mid = cube_at // group_mid
    place_mid = cube_at % group_mid
    front_leaf = cube_at // group_leaf
    place_leaf = cube_at % group_leaf
    size_root = front_blocks[0] * BLOCK_ROWS
    size_mid = front_blocks[1 + front_mid] * BLOCK_ROWS
    size_leaf = front_blocks[3 + front_leaf] * BLOCK_ROWS
    column_leaf = row_mask(first_row, slice_rows, size_leaf)
    column_mid = row_mask(first_row, slice_rows, size_mid)
    column_root = row_mask(first_row, slice_rows, size_root)
    own_leaf = pivot_leaf.shape[1]
    gathered = lax.dynamic_index_in_dim(rhs_leaf, front_leaf, 0, keepdims=False).astype(jnp.float32)
    solved_leaf, update_leaf = forward_front(
        pivot_leaf,
        coupling_leaf,
        gathered,
        column_leaf,
        row_mask(place_leaf * own_leaf, own_leaf, size_leaf),
    )
    own_mid = pivot_mid.shape[1]
    arrived = gather_bits(update_leaf, bits_mid, cube_at)
    targets = lax.dynamic_slice_in_dim(child_map, 2 + 2 * front_mid, 2, 0).reshape(-1)
    gathered = lax.dynamic_index_in_dim(rhs_mid, front_mid, 0, keepdims=False).astype(jnp.float32)
    gathered = gathered - extend_add(arrived, targets, first_block, slice_blocks)
    solved_mid, update_mid = forward_front(
        pivot_mid,
        coupling_mid,
        gathered,
        column_mid,
        row_mask(place_mid * own_mid, own_mid, size_mid),
    )
    own_root = pivot_root.shape[1]
    arrived = gather_bits(update_mid, bits_root, cube_at)
    targets = child_map[0:2].reshape(-1)
    gathered = rhs_root[0].astype(jnp.float32) - extend_add(
        arrived, targets, first_block, slice_blocks
    )
    solved_root, unused = forward_front(
        pivot_root, None, gathered, column_root, row_mask(cube_at * own_root, own_root, size_root)
    )
    total = lax.psum(complex_apply_t(pivot_root, solved_root), "cube")
    full_root = (column_root * total).astype(jnp.bfloat16)
    piece_root = slice_rows // cube_n
    answer_root = lax.dynamic_slice_in_dim(full_root, cube_at * piece_root, piece_root, 0)
    update_rows_mid = coupling_mid.shape[1]
    rows = place_mid * update_rows_mid + jnp.arange(update_rows_mid, dtype=jnp.int32)
    targets = lax.dynamic_slice_in_dim(child_map, front_mid, 1, 0).reshape(-1)
    pulled = blk_total(pick_rows(full_root, targets, rows, first_row)).astype(jnp.bfloat16)
    term = complex_apply_t(pivot_mid, solved_mid) - complex_apply_t(coupling_mid, pulled)
    piece_mid = slice_rows // group_mid
    share = halve_bits(term, bits_mid, cube_at)
    answer_mid = (row_mask(first_row + place_mid * piece_mid, piece_mid, size_mid) * share).astype(
        jnp.bfloat16
    )
    full_mid = gather_bits(answer_mid, bits_mid, cube_at)
    update_rows_leaf = coupling_leaf.shape[1]
    rows = place_leaf * update_rows_leaf + jnp.arange(update_rows_leaf, dtype=jnp.int32)
    targets = lax.dynamic_slice_in_dim(child_map, 2 + front_leaf, 1, 0).reshape(-1)
    pulled = blk_total(pick_rows(full_mid, targets, rows, first_row)).astype(jnp.bfloat16)
    term = complex_apply_t(pivot_leaf, solved_leaf) - complex_apply_t(coupling_leaf, pulled)
    piece_leaf = slice_rows // group_leaf
    share = halve_bits(term, bits_leaf, cube_at)
    answer_leaf = (
        row_mask(first_row + place_leaf * piece_leaf, piece_leaf, size_leaf) * share
    ).astype(jnp.bfloat16)
    return (answer_root[None], answer_mid[None], answer_leaf[None])


def solution(mesh):
    in_specs = (
        P(None, "blk", None),
        P(None, "blk", None),
        P(None, "blk", None),
        P(None, "cube", "blk"),
        P(None, "cube", "blk"),
        P(None, "cube", "blk"),
        P(None, "cube", "blk"),
        P(None, "cube", "blk"),
        P(),
        P(),
    )
    out_specs = (P("blk", "cube", None), P("blk", "cube", None), P("blk", "cube", None))
    return jax.shard_map(
        per_device, mesh=mesh, in_specs=in_specs, out_specs=out_specs, check_vma=False
    )
```

profile of v0, /device:TPU:0, one launch (start us, length us, event | category | flops | bytes accessed | tf_op | source)
XLA Modules:
  0.0 470.1 jit_solution(2196238573120029285)
XLA Ops:
  11.7 3.4 fusion.65
  15.3 2.7 fusion.111
  18.0 15.5 %fusion.2 = f32[128,5120]{1,0:T(8,128)} fusion(bf16[2,5120,2560]{2,1,0:T(8,128)(2,1)} %param.15, bf16[2560,64]{1,0:T(8,128)(2,1)S(1)} %get-tuple-element.24, bf16[2560,64]{1,0:T(8,128)(2,1)S(1)} %get-tuple-element.23), kind=kOutput, calls=%fused_computation.4 | convolution fusion | flops 3356753920 | bytes 29491200 | tf_op jit(solution)/shard_map/dot_general | solution.py:21
  33.6 15.2 %fusion.35 = f32[5120,128]{0,1:T(8,128)S(1)} fusion(f32[128,5120]{1,0:T(8,128)} %fusion.2, bf16[2,5120,2560]{2,1,0:T(8,128)(2,1)} %param.15, f32[2560]{0:T(1024)S(1)} %get-tuple-element.43, bf16[4,2560,128]{2,1,0:T(8,128)(2,1)} %param.12, s32[]{:T(128)S(6)} %select_n.217), kind=kOutput, calls=%fused_computation.35 | convolution fusion | flops 3357081600 | bytes 32122884 | tf_op jit(solution)/shard_map/dot_general | solution.py:20
  52.1 66.6 %all-reduce.7.cloned.1.call-done = f32[5760,128]{0,1:T(8,128)} async-done(((f32[5760,128]{0,1:T(8,128)}), f32[5760,128]{0,1:T(8,128)}) %all-reduce.7.cloned.1.call-update) | async-done | bytes 2949136 | tf_op jit(solution)/shard_map/psum | solution.py:63
  122.1 3.3 collective-permute-done
  127.2 6.7 %collective-permute-done.1 = bf16[1280,128]{0,1:T(8,128)(2,1)S(1)} collective-permute-done((bf16[1280,128]{0,1:T(8,128)(2,1)S(1)}, bf16[1280,128]{0,1:T(8,128)(2,1)S(1)}, u32[]{:S(2)}, u32[]{:S(2)}) %collective-permute-start.1) | collective-permute-done | bytes 327712 | tf_op jit(solution)/shard_map/ppermute | solution.py:11
  139.8 7.9 %fusion.14 = f32[128,2560]{1,0:T(8,128)S(1)} fusion(bf16[2,2560,2560]{2,1,0:T(8,128)(2,1)} %param.14, bf16[2560,64]{1,0:T(8,128)(2,1)S(1)} %get-tuple-element.22, bf16[2560,64]{1,0:T(8,128)(2,1)S(1)} %get-tuple-element.21), kind=kOutput, calls=%fused_computation.16 | convolution fusion | flops 1679032320 | bytes 15073280 | tf_op jit(solution)/shard_map/dot_general | solution.py:21
  147.7 7.4 %fusion.58 = f32[2560,128]{0,1:T(8,128)S(1)} fusion(f32[128,2560]{1,0:T(8,128)S(1)} %fusion.14, bf16[2560,128]{1,0:T(8,128)(2,1)S(1)} %bitcast.160, bf16[2,2560,2560]{2,1,0:T(8,128)(2,1)} %param.14), kind=kOutput, calls=%fused_computation.50 | convolution fusion | flops 1678049280 | bytes 16384000 | tf_op jit(solution)/shard_map/dot_general | solution.py:20
  159.8 40.0 %all-reduce.9.cloned.1.call-done = f32[2880,128]{0,1:T(8,128)} async-done(((f32[2880,128]{0,1:T(8,128)}), f32[2880,128]{0,1:T(8,128)}) %all-reduce.9.cloned.1.call-update) | async-done | bytes 1474576 | tf_op jit(solution)/shard_map/psum | solution.py:63
  202.2 3.1 collective-permute-done.2
  213.0 2.5 collective-permute-start.4
  217.1 11.0 %collective-permute-done.4 = bf16[1280,128]{0,1:T(8,128)(2,1)S(1)} collective-permute-done((bf16[1280,128]{0,1:T(8,128)(2,1)S(1)}, bf16[1280,128]{0,1:T(8,128)(2,1)S(1)}, u32[]{:S(2)}, u32[]{:S(2)}) %collective-permute-start.4) | collective-permute-done | bytes 327712 | tf_op jit(solution)/shard_map/ppermute | solution.py:11
  231.8 5.1 %fusion.26 = f32[128,1280]{1,0:T(8,128)S(1)} fusion(bf16[2,1280,2560]{2,1,0:T(8,128)(2,1)} %param.13, bf16[2560,64]{0,1:T(8,128)(2,1)S(1)} %get-tuple-element.20, bf16[2560,64]{0,1:T(8,128)(2,1)S(1)} %get-tuple-element.19), kind=kOutput, calls=%fused_computation.28 | convolution fusion | flops 840171520 | bytes 7864320 | tf_op jit(solution)/shard_map/dot_general | solution.py:21
  237.0 6.1 %fusion.79 = f32[1280,128]{0,1:T(8,128)} fusion(f32[128,1280]{1,0:T(8,128)S(1)} %fusion.26, bf16[2560,128]{1,0:T(8,128)(2,1)S(1)} %bitcast.162, bf16[2,1280,2560]{2,1,0:T(8,128)(2,1)} %param.13), kind=kOutput, calls=%fused_computation.67 | convolution fusion | flops 839024640 | bytes 8519680 | tf_op jit(solution)/shard_map/dot_general | solution.py:20
  243.2 34.1 %all-reduce.11.cloned.1.call-done = f32[1280,128]{0,1:T(8,128)} async-done(((f32[1280,128]{0,1:T(8,128)}), f32[1280,128]{0,1:T(8,128)}) %all-reduce.11.cloned.1.call-update) | async-done | bytes 655376 | tf_op jit(solution)/shard_map/psum | solution.py:63
  278.5 3.9 fusion.24
  282.3 5.0 %fusion.49 = f32[2560,128]{0,1:T(8,128)} fusion(f32[128,2560]{1,0:T(8,128)S(1)} %fusion.24, bf16[1280,128]{0,1:T(8,128)(2,1)S(1)} %multiply_convert_fusion.2, bf16[2,1280,2560]{2,1,0:T(8,128)(2,1)} %param.13), kind=kOutput, calls=%fused_computation.47 | convolution fusion | flops 839188480 | bytes 9502720 | tf_op jit(solution)/shard_map/dot_general | solution.py:27
  287.4 5.8 %fusion.12 = f32[128,2560]{1,0:T(8,128)S(1)} fusion(bf16[2,2560,2560]{2,1,0:T(8,128)(2,1)} %param.14, bf16[2560,64]{0,1:T(8,128)(2,1)S(1)} %get-tuple-element.18, bf16[2560,64]{0,1:T(8,128)(2,1)S(1)} %get-tuple-element.17), kind=kOutput, calls=%fused_computation.14 | convolution fusion | flops 1679032320 | bytes 15073280 | tf_op jit(solution)/shard_map/dot_general | solution.py:28
  293.2 7.7 %fusion.61 = f32[128,2560]{1,0:T(8,128)} fusion(f32[128,2560]{1,0:T(8,128)S(1)} %fusion.12, bf16[2560,128]{0,1:T(8,128)(2,1)S(1)} %copy-done.4, bf16[2,2560,2560]{2,1,0:T(8,128)(2,1)} %param.14), kind=kOutput, calls=%fused_computation.51 | convolution fusion | flops 1678049280 | bytes 16384000 | tf_op jit(solution)/shard_map/dot_general | solution.py:27
  300.8 70.3 %all-reduce.13.cloned.1.call-done = f32[2560,128]{0,1:T(8,128)} async-done(((f32[2560,128]{0,1:T(8,128)}), f32[2560,128]{0,1:T(8,128)}) %all-reduce.13.cloned.1.call-update) | async-done | bytes 1310736 | tf_op jit(solution)/shard_map/psum | solution.py:168
  371.2 2.4 multiply_convert_fusion
  375.7 2.3 gather_fusion
  378.1 13.4 %all-reduce.14 = bf16[320,128]{1,0:T(8,128)(2,1)S(1)} all-reduce(f32[320,128]{1,0:T(8,128)S(1)} %convert_select_fusion.1), channel_id=1, replica_groups=mesh['cube'=8,'blk'=4] {'blk'}, use_global_device_ids=true, to_apply=%region_5.6 | all-reduce | flops 40960 | bytes 245760 | tf_op jit(solution)/shard_map/psum | solution.py:63
  395.0 7.4 %collective-permute-done.5 = bf16[1280,128]{0,1:T(8,128)(2,1)S(1)} collective-permute-done((bf16[1280,128]{0,1:T(8,128)(2,1)S(1)}, bf16[1280,128]{0,1:T(8,128)(2,1)S(1)}, u32[]{:S(2)}, u32[]{:S(2)}) %collective-permute-start.5) | collective-permute-done | bytes 327712 | tf_op jit(solution)/shard_map/ppermute | solution.py:11
  404.1 4.0 collective-permute-done.6
  409.7 10.3 %fusion = f32[128,2560]{1,0:T(8,128)S(1)} fusion(bf16[2,5120,2560]{2,1,0:T(8,128)(2,1)} %param.15, bf16[5120,64]{0,1:T(8,128)(2,1)S(1)} %get-tuple-element.16, bf16[5120,64]{0,1:T(8,128)(2,1)S(1)} %get-tuple-element.15), kind=kOutput, calls=%fused_computation.2 | convolution fusion | flops 3358064640 | bytes 28835840 | tf_op jit(solution)/shard_map/dot_general | solution.py:28
  421.4 10.5 %fusion.52 = f32[128,2560]{1,0:T(8,128)S(1)} fusion(f32[128,2560]{1,0:T(8,128)S(1)} %fusion, bf16[5120,128]{0,1:T(8,128)(2,1)S(1)} %fusion.75, bf16[2,5120,2560]{2,1,0:T(8,128)(2,1)} %param.15), kind=kOutput, calls=%fused_computation.48 | convolution fusion | flops 3355770880 | bytes 30146560 | tf_op jit(solution)/shard_map/dot_general | solution.py:27
  434.7 14.0 %all-reduce.15 = bf16[640,128]{1,0:T(8,128)(2,1)S(1)} all-reduce(f32[640,128]{1,0:T(8,128)S(1)} %convert_select_fusion), channel_id=1, replica_groups=mesh['cube'=8,'blk'=4] {'blk'}, use_global_device_ids=true, to_apply=%region_7.8 | all-reduce | flops 81920 | bytes 491520 | tf_op jit(solution)/shard_map/psum | solution.py:63
  448.9 2.6 fusion.67
  451.5 2.7 fusion.45
  457.4 4.9 %collective-permute-done.9 = bf16[1280,128]{0,1:T(8,128)(2,1)S(1)} collective-permute-done((bf16[1280,128]{0,1:T(8,128)(2,1)S(1)}, bf16[1280,128]{0,1:T(8,128)(2,1)S(1)}, u32[]{:S(2)}, u32[]{:S(2)}) %collective-permute-start.9) | collective-permute-done | bytes 327712 | tf_op jit(solution)/shard_map/ppermute | solution.py:11
  (143 shorter events, 55.6 us)
Async XLA Ops:
  7.2 111.5 %all-reduce.7.cloned.1.call-start = ((), (), s32[]{:S(2)}) async-start(), calls=%async_computation | async-start | bytes 5898240 | tf_op jit(solution)/shard_map/psum | solution.py:63
  11.4 3.8 copy-start
  50.5 1.2 copy-start.16
  50.5 76.5 %copy-start.6 = (bf16[2,2560,128]{2,1,0:T(8,128)(2,1)S(1)}, bf16[2,2560,128]{2,1,0:T(8,128)(2,1)}, u32[]{:S(2)}) copy-start(bf16[2,2560,128]{2,1,0:T(8,128)(2,1)} %param.11) | copy-start | bytes 3932164
  50.6 149.2 %all-reduce.9.cloned.1.call-start = ((), (), s32[]{:S(2)}) async-start(), calls=%async_computation.1 | async-start | bytes 3014656 | tf_op jit(solution)/shard_map/psum | solution.py:63
  119.7 5.7 %collective-permute-start = (bf16[640,128]{0,1:T(8,128)(2,1)S(1)}, bf16[640,128]{0,1:T(8,128)(2,1)S(1)}, u32[]{:S(2)}, u32[]{:S(2)}) collective-permute-start(bf16[640,128]{0,1:T(8,128)(2,1)S(1)} %slice.339), channel_id=1, source_target_pairs={{0,4},{4,0},{8,12},{12,8},{16,20},{20,16},{24,28},{28,24},{1,5},{5... | collective-permute-start | bytes 491528 | tf_op jit(solution)/shard_map/ppermute | solution.py:11
  125.5 8.4 %collective-permute-start.1 = (bf16[1280,128]{0,1:T(8,128)(2,1)S(1)}, bf16[1280,128]{0,1:T(8,128)(2,1)S(1)}, u32[]{:S(2)}, u32[]{:S(2)}) collective-permute-start(bf16[1280,128]{0,1:T(8,128)(2,1)S(1)} %maximum_select_fusion.3), channel_id=1, source_target_pairs={{0,8},{4,12},{8,0},{12,4},{16,24},{20,28},{24,16},{28,20},{1,9},{5... | collective-permute-start | bytes 983048 | tf_op jit(solution)/shard_map/ppermute | solution.py:11
  135.9 1.3 copy-start.7
  137.2 1.9 copy-start.1
  157.1 51.8 %copy-start.9 = (bf16[1,2560,128]{2,1,0:T(8,128)(2,1)S(1)}, bf16[1,2560,128]{2,1,0:T(8,128)(2,1)}, u32[]{:S(2)}) copy-start(bf16[1,2560,128]{2,1,0:T(8,128)(2,1)} %param.10) | copy-start | bytes 1966084
  157.2 120.1 %all-reduce.11.cloned.1.call-start = ((), (), s32[]{:S(2)}) async-start(), calls=%async_computation.2 | async-start | bytes 1310720 | tf_op jit(solution)/shard_map/psum | solution.py:63
  200.7 4.7 collective-permute-start.2
  206.2 5.6 %collective-permute-start.3 = (bf16[640,128]{0,1:T(8,128)(2,1)}, bf16[640,128]{0,1:T(8,128)(2,1)}, u32[]{:S(2)}, u32[]{:S(2)}) collective-permute-start(bf16[640,128]{0,1:T(8,128)(2,1)} %maximum_select_fusion.6), channel_id=1, source_target_pairs={{0,8},{4,12},{8,0},{12,4},{16,24},{20,28},{24,16},{28,20},{1,9},{5... | collective-permute-start | bytes 491528 | tf_op jit(solution)/shard_map/ppermute | solution.py:11
  209.2 6.3 %copy-start.5 = (f32[2880,128]{0,1:T(8,128)S(1)}, f32[2880,128]{0,1:T(8,128)}, u32[]{:S(2)}) copy-start(f32[2880,128]{0,1:T(8,128)} %all-reduce.9.cloned.1.call-done) | copy-start | bytes 4423684
  213.0 15.1 %collective-permute-start.4 = (bf16[1280,128]{0,1:T(8,128)(2,1)S(1)}, bf16[1280,128]{0,1:T(8,128)(2,1)S(1)}, u32[]{:S(2)}, u32[]{:S(2)}) collective-permute-start(bf16[1280,128]{0,1:T(8,128)(2,1)S(1)} %maximum_select_fusion.4), channel_id=1, source_target_pairs={{0,16},{4,20},{8,24},{12,28},{16,0},{20,4},{24,8},{28,12},{1,17},{... | collective-permute-start | bytes 983048 | tf_op jit(solution)/shard_map/ppermute | solution.py:11
  217.1 11.5 %copy-start.18 = (s32[20]{0:T(128)S(1)}, s32[20]{0:T(128)}, u32[]{:S(2)}) copy-start(s32[20]{0:T(128)} %sub.112) | copy-start | bytes 244
  231.8 5.1 %copy-start.10 = (bf16[20,128,128]{2,1,0:T(8,128)(2,1)S(1)}, bf16[20,128,128]{2,1,0:T(8,128)(2,1)}, u32[]{:S(2)}) copy-start(bf16[20,128,128]{2,1,0:T(8,128)(2,1)} %copy.75) | copy-start | bytes 1966084
  236.9 6.2 %copy-start.4 = (bf16[2560,128]{0,1:T(8,128)(2,1)S(1)}, bf16[2560,128]{0,1:T(8,128)(2,1)}, u32[]{:S(2)}) copy-start(bf16[2560,128]{0,1:T(8,128)(2,1)} %fusion.100) | copy-start | bytes 1966084
  243.1 34.2 %copy-start.12 = (f32[1280]{0:T(1024)S(1)}, f32[1280]{0:T(1024)}, u32[]{:S(2)}) copy-start(f32[1280]{0:T(1024)} %fusion.159) | copy-start | bytes 15364
  243.1 128.1 %all-reduce.13.cloned.1.call-start = ((), (), s32[]{:S(2)}) async-start(), calls=%async_computation.3 | async-start | bytes 2621440 | tf_op jit(solution)/shard_map/psum | solution.py:168
  300.8 74.9 %copy-start.14 = (s32[1024]{0:T(1024)S(1)}, s32[1024]{0:T(1024)}, u32[]{:S(2)}) copy-start(s32[1024]{0:T(1024)} %pad_clamp_fusion.1) | copy-start | bytes 12292
  371.1 20.5 %copy-start.2 = (bf16[2,320,2560]{2,1,0:T(8,128)(2,1)S(1)}, bf16[2,320,2560]{2,1,0:T(8,128)(2,1)}, u32[]{:S(2)}) copy-start(bf16[2,320,2560]{2,1,0:T(8,128)(2,1)} %param.16) | copy-start | bytes 9830404
  373.5 4.5 copy-start.17
  391.6 1.3 copy-start.8
  392.9 1.8 copy-start.3
  392.9 1.8 copy-start.11
  393.6 8.7 %collective-permute-start.5 = (bf16[1280,128]{0,1:T(8,128)(2,1)S(1)}, bf16[1280,128]{0,1:T(8,128)(2,1)S(1)}, u32[]{:S(2)}, u32[]{:S(2)}) collective-permute-start(bf16[1280,128]{0,1:T(8,128)(2,1)S(1)} %select_convert_fusion.1), channel_id=1, source_target_pairs={{0,8},{4,12},{8,0},{12,4},{16,24},{20,28},{24,16},{28,20},{1,9},{5... | collective-permute-start | bytes 983048 | tf_op jit(solution)/shard_map/ppermute | solution.py:11
  402.5 5.6 %collective-permute-start.6 = (bf16[640,128]{0,1:T(8,128)(2,1)S(1)}, bf16[640,128]{0,1:T(8,128)(2,1)S(1)}, u32[]{:S(2)}, u32[]{:S(2)}) collective-permute-start(bf16[640,128]{0,1:T(8,128)(2,1)S(1)} %select_convert_fusion.2), channel_id=1, source_target_pairs={{0,4},{4,0},{8,12},{12,8},{16,20},{20,16},{24,28},{28,24},{1,5},{5... | collective-permute-start | bytes 491528 | tf_op jit(solution)/shard_map/ppermute | solution.py:11
  408.2 11.9 %collective-permute-start.7 = (bf16[640,128]{0,1:T(8,128)(2,1)S(1)}, bf16[640,128]{0,1:T(8,128)(2,1)S(1)}, u32[]{:S(2)}, u32[]{:S(2)}) collective-permute-start(bf16[640,128]{0,1:T(8,128)(2,1)S(1)} %multiply_convert_fusion.3), channel_id=1, source_target_pairs={{0,4},{4,0},{8,12},{12,8},{16,20},{20,16},{24,28},{28,24},{1,5},{5... | collective-permute-start | bytes 491528 | tf_op jit(solution)/shard_map/ppermute | solution.py:11
  420.2 11.7 %collective-permute-start.8 = (bf16[1280,128]{0,1:T(8,128)(2,1)S(1)}, bf16[1280,128]{0,1:T(8,128)(2,1)S(1)}, u32[]{:S(2)}, u32[]{:S(2)}) collective-permute-start(bf16[1280,128]{0,1:T(8,128)(2,1)S(1)} %maximum_select_fusion.5), channel_id=1, source_target_pairs={{0,8},{4,12},{8,0},{12,4},{16,24},{20,28},{24,16},{28,20},{1,9},{5... | collective-permute-start | bytes 983048 | tf_op jit(solution)/shard_map/ppermute | solution.py:11
  432.1 2.5 copy-start.15
  454.3 8.0 %collective-permute-start.9 = (bf16[1280,128]{0,1:T(8,128)(2,1)S(1)}, bf16[1280,128]{0,1:T(8,128)(2,1)S(1)}, u32[]{:S(2)}, u32[]{:S(2)}) collective-permute-start(bf16[1280,128]{0,1:T(8,128)(2,1)S(1)} %select_convert_fusion), channel_id=1, source_target_pairs={{0,4},{4,0},{8,12},{12,8},{16,20},{20,16},{24,28},{28,24},{1,5},{5... | collective-permute-start | bytes 983048 | tf_op jit(solution)/shard_map/ppermute | solution.py:11
  (1 other events, 0.7 us)
Sparse Core Ops, SparseCore 0:
  50.7 67.9 all-reduce.6
  157.3 42.4 all-reduce.8
  243.2 34.0 all-reduce.10
  287.5 83.6 all-reduce.12
where the time goes:
time: 478 us; the launch traced here: 470 us
  waiting for transfers between devices  253 us (53%)
  matrix products  117 us (24%)
  blocking collectives  27.4 us (6%)
  local copies, waits for them, and re-layouts  22.2 us (5%)
  other arithmetic  19.3 us (4%)
  between operations  16.7 us (3%)
  starting transfers between devices  14.3 us (3%)
    psum x3, waiting for transfers between devices, blk_total(): return lax.psum(value, 'blk')  141 us
    psum x1, waiting for transfers between devices, per_device(): total = lax.psum(complex_apply_t(pivot_root, solved_root), 'cube')  70.3 us
    ppermute x10, waiting for transfers between devices, swapped(): lax.ppermute(value, axis, [(i, i ^ 1 << distance) for i in range(lax.axis...  42.2 us
    dot_general x5, matrix products, complex_apply(): jnp.dot(matrix[1], rotate_parts(vec), preferred_element_type=jnp.float32)  32.6 us
    dot_general x5, matrix products, complex_apply(): first = jnp.dot(matrix[0], vec, preferred_element_type=jnp.float32)  32 us
    psum x2, blocking collectives, blk_total(): return lax.psum(value, 'blk')  27.4 us
    dot_general x5, matrix products, complex_apply_t(): lax.dot_general(matrix[0], vec, dims, preferred_element_type=jnp.float32)  26.3 us
    dot_general x5, matrix products, complex_apply_t(): lax.dot_general(matrix[1], rotate_parts(vec), dims, preferred_element_typ...  23.4 us
  transfers between devices with their start and end apart: 14, of which 12 were waited for; matrix products, arithmetic and copies ran while one was open for 10% of the time, Pallas kernels for 0%

commit v1 on v0

--- a/solution.py
+++ b/solution.py
@@ -60,7 +60,7 @@
 
 
 def blk_total(value):
-    return lax.psum(value, "blk")
+    return jnp.sum(lax.all_gather(value, "blk"), axis=0)
 
 
 def row_mask(start, count, limit):

time: 478 us -> 540 us (1.13)
  matrix products: 117 us -> 142 us
  other arithmetic: 19.3 us -> 42 us
  local copies, waits for them, and re-layouts: 22.2 us -> 43.4 us
  blocking collectives: 27.4 us -> 8.31 us
  waiting for transfers between devices: 253 us -> 262 us
    all_gather x0 -> x4, waiting for transfers between devices: none -> 148 us  [blk_total(): return jnp.sum(lax.all_gather(value, 'blk'), axis=0)]
    psum x3 -> x0, waiting for transfers between devices: 141 us -> none  [blk_total(): return lax.psum(value, 'blk')]
    psum x2 -> x0, blocking collectives: 27.4 us -> none  [blk_total(): return lax.psum(value, 'blk')]
    reduce_sum x0 -> x5, other arithmetic: none -> 20.7 us  [blk_total(): return jnp.sum(lax.all_gather(value, 'blk'), axis=0)]
    all_gather x0 -> x2, local copies, waits for them, and re-layouts: none -> 17.2 us  [blk_total(): return jnp.sum(lax.all_gather(value, 'blk'), axis=0)]
    dot_general x5, matrix products: 23.4 us -> 34.7 us  [complex_apply_t(): lax.dot_general(matrix[1], rotate_parts(vec), dims, preferred_element_typ...]
    dot_general x5, matrix products: 26.3 us -> 34.8 us  [complex_apply_t(): lax.dot_general(matrix[0], vec, dims, preferred_element_type=jnp.float32)]
    all_gather x0 -> x1, blocking collectives: none -> 8.31 us  [blk_total(): return jnp.sum(lax.all_gather(value, 'blk'), axis=0)]
  transfers between devices with their start and end apart: 14 -> 15, of which waited for: 12 -> 14; matrix products, arithmetic and copies ran while one was open for 10% -> 11% of each run, Pallas kernels for 0% -> 0%
where the time goes in v1:
time: 540 us; the launch traced here: 531 us
  waiting for transfers between devices  262 us (49%)
  matrix products  142 us (26%)
  local copies, waits for them, and re-layouts  43.4 us (8%)
  other arithmetic  42 us (8%)
  starting transfers between devices  16.8 us (3%)
  between operations  16.7 us (3%)
  blocking collectives  8.31 us (2%)
    all_gather x4, waiting for transfers between devices, blk_total(): return jnp.sum(lax.all_gather(value, 'blk'), axis=0)  148 us
    psum x1, waiting for transfers between devices, per_device(): total = lax.psum(complex_apply_t(pivot_root, solved_root), 'cube')  64.2 us
    ppermute x10, waiting for transfers between devices, swapped(): lax.ppermute(value, axis, [(i, i ^ 1 << distance) for i in range(lax.axis...  50.2 us
    dot_general x5, matrix products, complex_apply(): first = jnp.dot(matrix[0], vec, preferred_element_type=jnp.float32)  35.8 us
    dot_general x5, matrix products, complex_apply_t(): lax.dot_general(matrix[0], vec, dims, preferred_element_type=jnp.float32)  34.8 us
    dot_general x5, matrix products, complex_apply_t(): lax.dot_general(matrix[1], rotate_parts(vec), dims, preferred_element_typ...  34.7 us
    dot_general x5, matrix products, complex_apply(): jnp.dot(matrix[1], rotate_parts(vec), preferred_element_type=jnp.float32)  32.9 us
    reduce_sum x5, other arithmetic, blk_total(): return jnp.sum(lax.all_gather(value, 'blk'), axis=0)  20.7 us
  transfers between devices with their start and end apart: 15, of which 14 were waited for; matrix products, arithmetic and copies ran while one was open for 11% of the time, Pallas kernels for 0%

profile of v1, /device:TPU:0, one launch (start us, length us, event | category | flops | bytes accessed | tf_op | source)
XLA Modules:
  0.0 531.1 jit_solution(1609403822463187938)
XLA Ops:
  12.8 15.5 %fusion.2 = f32[128,5120]{1,0:T(8,128)} fusion(bf16[2,5120,2560]{2,1,0:T(8,128)(2,1)} %param.15, bf16[2560,64]{1,0:T(8,128)(2,1)S(1)} %get-tuple-element.24, bf16[2560,64]{1,0:T(8,128)(2,1)S(1)} %get-tuple-element.23), kind=kOutput, calls=%fused_computation.4 | convolution fusion | flops 3356753920 | bytes 29491200 | tf_op jit(solution)/shard_map/dot_general | solution.py:21
  28.3 15.2 %fusion.35 = f32[5120,128]{0,1:T(8,128)S(1)} fusion(f32[128,5120]{1,0:T(8,128)} %fusion.2, bf16[2,5120,2560]{2,1,0:T(8,128)(2,1)} %param.15, f32[2560]{0:T(1024)S(1)} %get-tuple-element.43, bf16[4,2560,128]{2,1,0:T(8,128)(2,1)} %param.12, s32[]{:T(128)S(6)} %select_n.231), kind=kOutput, calls=%fused_computation.35 | convolution fusion | flops 3357081600 | bytes 32122884 | tf_op jit(solution)/shard_map/dot_general | solution.py:20
  43.4 3.6 fusion.65
  47.1 3.8 fusion.111
  53.7 79.6 %all-gather.10.cloned.1.call-done = f32[23040,128]{0,1:T(8,128)} async-done(((f32[5760,128]{0,1:T(8,128)}), f32[23040,128]{0,1:T(8,128)}) %all-gather.10.cloned.1.call-update) | async-done | bytes 11796496 | tf_op jit(solution)/shard_map/all_gather | solution.py:63
  133.3 13.2 %reshape.408 = f32[4,5760,128]{1,0,2:T(4,128)} reshape(f32[23040,128]{0,1:T(8,128)} %all-gather.10.cloned.1.call-done) | data formatting | bytes 23592960 | tf_op jit(solution)/shard_map/all_gather | solution.py:63
  146.5 9.8 %reduce_sum.63 = f32[5760,128]{0,1:T(8,128)S(1)} reduce(f32[4,5760,128]{1,0,2:T(4,128)} %reshape.408, f32[]{:T(128)} %constant.135.clone.1), dimensions={0}, to_apply=%region_0.1 | reduce | flops 2211840 | bytes 14745604 | tf_op jit(solution)/shard_map/reduce_sum | solution.py:63
  158.2 4.7 collective-permute-done
  165.7 6.3 %collective-permute-done.1 = bf16[1280,128]{1,0:T(8,128)(2,1)S(1)} collective-permute-done((bf16[1280,128]{1,0:T(8,128)(2,1)S(1)}, bf16[1280,128]{1,0:T(8,128)(2,1)S(1)}, u32[]{:S(2)}, u32[]{:S(2)}) %collective-permute-start.1) | collective-permute-done | bytes 327712 | tf_op jit(solution)/shard_map/ppermute | solution.py:11
  175.7 8.1 %fusion.14 = f32[128,2560]{1,0:T(8,128)S(1)} fusion(bf16[2,2560,2560]{2,1,0:T(8,128)(2,1)} %param.14, bf16[2560,64]{1,0:T(8,128)(2,1)S(1)} %get-tuple-element.22, bf16[2560,64]{1,0:T(8,128)(2,1)S(1)} %get-tuple-element.21), kind=kOutput, calls=%fused_computation.16 | convolution fusion | flops 1679032320 | bytes 15073280 | tf_op jit(solution)/shard_map/dot_general | solution.py:21
  184.5 10.2 %fusion.58 = f32[2560,128]{0,1:T(8,128)} fusion(f32[128,2560]{1,0:T(8,128)S(1)} %fusion.14, bf16[2560,128]{1,0:T(8,128)(2,1)S(1)} %bitcast.171, bf16[2,2560,2560]{2,1,0:T(8,128)(2,1)} %param.14), kind=kOutput, calls=%fused_computation.50 | convolution fusion | flops 1678049280 | bytes 16384000 | tf_op jit(solution)/shard_map/dot_general | solution.py:20
  201.2 44.0 %all-gather.12.cloned.1.call-done = f32[11520,128]{1,0:T(8,128)} async-done(((f32[2880,128]{1,0:T(8,128)}), f32[11520,128]{1,0:T(8,128)}) %all-gather.12.cloned.1.call-update) | async-done | bytes 5898256 | tf_op jit(solution)/shard_map/all_gather | solution.py:63
  245.3 4.3 reduce_sum.64
  256.7 4.0 collective-permute-done.3
  268.0 9.0 %collective-permute-done.4 = bf16[1280,128]{1,0:T(8,128)(2,1)} collective-permute-done((bf16[1280,128]{1,0:T(8,128)(2,1)S(1)}, bf16[1280,128]{1,0:T(8,128)(2,1)}, u32[]{:S(2)}, u32[]{:S(2)}) %collective-permute-start.4) | collective-permute-done | bytes 327712 | tf_op jit(solution)/shard_map/ppermute | solution.py:11
  286.5 5.0 fusion.26
  291.6 6.0 %fusion.79 = f32[1280,128]{0,1:T(8,128)} fusion(f32[128,1280]{1,0:T(8,128)S(1)} %fusion.26, bf16[2560,128]{1,0:T(8,128)(2,1)S(1)} %bitcast.173, bf16[2,1280,2560]{2,1,0:T(8,128)(2,1)} %param.13), kind=kOutput, calls=%fused_computation.67 | convolution fusion | flops 839024640 | bytes 8519680 | tf_op jit(solution)/shard_map/dot_general | solution.py:20
  302.0 21.2 %all-gather.14.cloned.1.call-done = f32[5120,128]{0,1:T(8,128)} async-done(((f32[1280,128]{0,1:T(8,128)}), f32[5120,128]{0,1:T(8,128)}) %all-gather.14.cloned.1.call-update) | async-done | bytes 2621456 | tf_op jit(solution)/shard_map/all_gather | solution.py:63
  323.3 3.9 reshape.410
  327.2 4.2 reduce_sum.65
  332.6 3.9 fusion.24
  336.5 5.0 fusion.49
  341.9 9.1 %fusion.12 = f32[128,2560]{0,1:T(8,128)S(1)} fusion(bf16[2,2560,2560]{2,1,0:T(8,128)(2,1)} %param.14, bf16[2560,64]{1,0:T(8,128)(2,1)} %get-tuple-element.18, bf16[2560,64]{1,0:T(8,128)(2,1)} %get-tuple-element.17), kind=kOutput, calls=%fused_computation.14 | convolution fusion | flops 1679032320 | bytes 15728640 | tf_op jit(solution)/shard_map/dot_general | solution.py:28
  351.0 10.0 %fusion.61 = f32[128,2560]{0,1:T(8,128)} fusion(f32[128,2560]{0,1:T(8,128)S(1)} %fusion.12, bf16[2560,128]{1,0:T(8,128)(2,1)S(1)} %copy-done.2, bf16[2,2560,2560]{2,1,0:T(8,128)(2,1)} %param.14), kind=kOutput, calls=%fused_computation.51 | convolution fusion | flops 1678049280 | bytes 16384000 | tf_op jit(solution)/shard_map/dot_general | solution.py:27
  361.0 64.2 %all-reduce.2.cloned.1.call-done = f32[2560,128]{0,1:T(8,128)} async-done(((f32[2560,128]{0,1:T(8,128)}), f32[2560,128]{0,1:T(8,128)}) %all-reduce.2.cloned.1.call-update) | async-done | bytes 1310736 | tf_op jit(solution)/shard_map/psum | solution.py:168
  432.1 8.3 %all_gather.32 = f32[4,320,128]{2,1,0:T(8,128)} all-gather(f32[1,320,128]{2,1,0:T(8,128)S(1)} %convert_select_fusion.1), channel_id=1, replica_groups=mesh['cube'=8,'blk'=4] {'blk'}, dimensions={0}, use_global_device_ids=true | all-gather | bytes 819200 | tf_op jit(solution)/shard_map/all_gather | solution.py:63
  447.8 8.7 %collective-permute-done.5 = bf16[1280,128]{1,0:T(8,128)(2,1)S(1)} collective-permute-done((bf16[1280,128]{1,0:T(8,128)(2,1)S(1)}, bf16[1280,128]{1,0:T(8,128)(2,1)S(1)}, u32[]{:S(2)}, u32[]{:S(2)}) %collective-permute-start.5) | collective-permute-done | bytes 327712 | tf_op jit(solution)/shard_map/ppermute | solution.py:11
  458.4 3.9 collective-permute-done.6
  464.1 3.7 collective-permute-done.7
  469.2 16.1 %fusion = f32[128,2560]{0,1:T(8,128)} fusion(bf16[2,5120,2560]{2,1,0:T(8,128)(2,1)} %param.15, bf16[5120,64]{0,1:T(8,128)(2,1)S(1)} %get-tuple-element.16, bf16[5120,64]{0,1:T(8,128)(2,1)S(1)} %get-tuple-element.15), kind=kOutput, calls=%fused_computation.2 | convolution fusion | flops 3358064640 | bytes 28835840 | tf_op jit(solution)/shard_map/dot_general | solution.py:28
  488.4 14.0 %fusion.52 = f32[128,2560]{0,1:T(8,128)} fusion(f32[128,2560]{0,1:T(8,128)} %fusion, bf16[5120,128]{0,1:T(8,128)(2,1)S(1)} %copy-done.4, bf16[2,5120,2560]{2,1,0:T(8,128)(2,1)} %param.15), kind=kOutput, calls=%fused_computation.48 | convolution fusion | flops 3355770880 | bytes 30146560 | tf_op jit(solution)/shard_map/dot_general | solution.py:27
  516.8 6.6 %collective-permute-done.9 = bf16[1280,128]{1,0:T(8,128)(2,1)S(1)} collective-permute-done((bf16[1280,128]{1,0:T(8,128)(2,1)S(1)}, bf16[1280,128]{1,0:T(8,128)(2,1)S(1)}, u32[]{:S(2)}, u32[]{:S(2)}) %collective-permute-start.9) | collective-permute-done | bytes 327712 | tf_op jit(solution)/shard_map/ppermute | solution.py:11
  (139 shorter events, 89.2 us)
Async XLA Ops:
  7.2 126.1 %all-gather.10.cloned.1.call-start = ((), (), s32[]{:S(2)}) async-start(), calls=%async_computation.2 | async-start | bytes 14745600 | tf_op jit(solution)/shard_map/all_gather | solution.py:63
  11.7 0.8 copy-start.10
  11.7 1.0 copy-start.11
  52.7 0.9 copy-start.13
  52.8 192.5 %all-gather.12.cloned.1.call-start = ((), (), s32[]{:S(2)}) async-start(), calls=%async_computation.3 | async-start | bytes 7372800 | tf_op jit(solution)/shard_map/all_gather | solution.py:63
  156.5 6.4 %collective-permute-start = (bf16[640,128]{1,0:T(8,128)(2,1)S(1)}, bf16[640,128]{1,0:T(8,128)(2,1)S(1)}, u32[]{:S(2)}, u32[]{:S(2)}) collective-permute-start(bf16[640,128]{1,0:T(8,128)(2,1)S(1)} %copy.146), channel_id=1, source_target_pairs={{0,4},{4,0},{8,12},{12,8},{16,20},{20,16},{24,28},{28,24},{1,5},{5... | collective-permute-start | bytes 491528 | tf_op jit(solution)/shard_map/ppermute | solution.py:11
  163.0 9.1 %collective-permute-start.1 = (bf16[1280,128]{1,0:T(8,128)(2,1)S(1)}, bf16[1280,128]{1,0:T(8,128)(2,1)S(1)}, u32[]{:S(2)}, u32[]{:S(2)}) collective-permute-start(bf16[1280,128]{1,0:T(8,128)(2,1)S(1)} %maximum_select_fusion.3), channel_id=1, source_target_pairs={{0,8},{4,12},{8,0},{12,4},{16,24},{20,28},{24,16},{28,20},{1,9},{5... | collective-permute-start | bytes 983048 | tf_op jit(solution)/shard_map/ppermute | solution.py:11
  173.6 1.3 copy-start.9
  175.7 8.1 %copy-start.5 = (bf16[2,320,2560]{2,1,0:T(8,128)(2,1)S(1)}, bf16[2,320,2560]{2,1,0:T(8,128)(2,1)}, u32[]{:S(2)}) copy-start(bf16[2,320,2560]{2,1,0:T(8,128)(2,1)} %param.16) | copy-start | bytes 9830404
  201.0 122.3 %all-gather.14.cloned.1.call-start = ((), (), s32[]{:S(2)}) async-start(), calls=%async_computation.4 | async-start | bytes 3276800 | tf_op jit(solution)/shard_map/all_gather | solution.py:63
  250.4 4.7 collective-permute-start.2
  255.2 5.6 %collective-permute-start.3 = (bf16[640,128]{1,0:T(8,128)(2,1)S(1)}, bf16[640,128]{1,0:T(8,128)(2,1)S(1)}, u32[]{:S(2)}, u32[]{:S(2)}) collective-permute-start(bf16[640,128]{1,0:T(8,128)(2,1)S(1)} %maximum_select_fusion.6), channel_id=1, source_target_pairs={{0,8},{4,12},{8,0},{12,4},{16,24},{20,28},{24,16},{28,20},{1,9},{5... | collective-permute-start | bytes 491528 | tf_op jit(solution)/shard_map/ppermute | solution.py:11
  260.8 16.2 %collective-permute-start.4 = (bf16[1280,128]{1,0:T(8,128)(2,1)S(1)}, bf16[1280,128]{1,0:T(8,128)(2,1)}, u32[]{:S(2)}, u32[]{:S(2)}) collective-permute-start(bf16[1280,128]{1,0:T(8,128)(2,1)S(1)} %maximum_select_fusion.4), channel_id=1, source_target_pairs={{0,16},{4,20},{8,24},{12,28},{16,0},{20,4},{24,8},{28,12},{1,17},{... | collective-permute-start | bytes 983048 | tf_op jit(solution)/shard_map/ppermute | solution.py:11
  268.0 10.3 %copy-start = (f32[1,2560,128]{2,1,0:T(8,128)S(1)}, f32[1,2560,128]{2,1,0:T(8,128)}, u32[]{:S(2)}) copy-start(f32[1,2560,128]{2,1,0:T(8,128)} %copy.114) | copy-start | bytes 3932164
  284.6 1.8 copy-start.7
  297.6 127.6 %all-reduce.2.cloned.1.call-start = ((), (), s32[]{:S(2)}) async-start(), calls=%async_computation | async-start | bytes 2621440 | tf_op jit(solution)/shard_map/psum | solution.py:168
  299.9 0.9 copy-start.1
  341.4 163.8 %all-gather.8.cloned.1.call-start = ((), (), s32[]{:S(2)}) async-start(), calls=%async_computation.1 | async-start | bytes 1638400 | tf_op jit(solution)/shard_map/all_gather | solution.py:63
  341.9 9.1 %copy-start.2 = (bf16[2560,128]{1,0:T(8,128)(2,1)S(1)}, bf16[2560,128]{1,0:T(8,128)(2,1)}, u32[]{:S(2)}) copy-start(bf16[2560,128]{1,0:T(8,128)(2,1)} %copy-done.1) | copy-start | bytes 1966084
  441.5 2.6 copy-start.6
  446.5 10.0 %collective-permute-start.5 = (bf16[1280,128]{1,0:T(8,128)(2,1)S(1)}, bf16[1280,128]{1,0:T(8,128)(2,1)S(1)}, u32[]{:S(2)}, u32[]{:S(2)}) collective-permute-start(bf16[1280,128]{1,0:T(8,128)(2,1)S(1)} %select_convert_fusion.1), channel_id=1, source_target_pairs={{0,8},{4,12},{8,0},{12,4},{16,24},{20,28},{24,16},{28,20},{1,9},{5... | collective-permute-start | bytes 983048 | tf_op jit(solution)/shard_map/ppermute | solution.py:11
  456.6 5.7 %collective-permute-start.6 = (bf16[640,128]{1,0:T(8,128)(2,1)S(1)}, bf16[640,128]{1,0:T(8,128)(2,1)S(1)}, u32[]{:S(2)}, u32[]{:S(2)}) collective-permute-start(bf16[640,128]{1,0:T(8,128)(2,1)S(1)} %select_convert_fusion.2), channel_id=1, source_target_pairs={{0,4},{4,0},{8,12},{12,8},{16,20},{20,16},{24,28},{28,24},{1,5},{5... | collective-permute-start | bytes 491528 | tf_op jit(solution)/shard_map/ppermute | solution.py:11
  458.4 5.7 %copy-start.3 = (bf16[5120,128]{0,1:T(8,128)(2,1)}, bf16[5120,128]{0,1:T(8,128)(2,1)S(1)}, u32[]{:S(2)}) copy-start(bf16[5120,128]{0,1:T(8,128)(2,1)S(1)} %fusion.75) | copy-start | bytes 3932164
  462.5 5.5 %copy-start.12 = (bf16[640,128]{1,0:T(8,128)(2,1)}, bf16[640,128]{1,0:T(8,128)(2,1)S(1)}, u32[]{:S(2)}) copy-start(bf16[640,128]{1,0:T(8,128)(2,1)S(1)} %multiply_convert_fusion.3) | copy-start | bytes 491524
  462.5 5.4 %collective-permute-start.7 = (bf16[640,128]{1,0:T(8,128)(2,1)S(1)}, bf16[640,128]{1,0:T(8,128)(2,1)S(1)}, u32[]{:S(2)}, u32[]{:S(2)}) collective-permute-start(bf16[640,128]{1,0:T(8,128)(2,1)S(1)} %multiply_convert_fusion.3), channel_id=1, source_target_pairs={{0,4},{4,0},{8,12},{12,8},{16,20},{20,16},{24,28},{28,24},{1,5},{5... | collective-permute-start | bytes 491528 | tf_op jit(solution)/shard_map/ppermute | solution.py:11
  468.0 17.4 %collective-permute-start.8 = (bf16[1280,128]{1,0:T(8,128)(2,1)S(1)}, bf16[1280,128]{1,0:T(8,128)(2,1)S(1)}, u32[]{:S(2)}, u32[]{:S(2)}) collective-permute-start(bf16[1280,128]{1,0:T(8,128)(2,1)S(1)} %maximum_select_fusion.5), channel_id=1, source_target_pairs={{0,8},{4,12},{8,0},{12,4},{16,24},{20,28},{24,16},{28,20},{1,9},{5... | collective-permute-start | bytes 983048 | tf_op jit(solution)/shard_map/ppermute | solution.py:11
  485.5 2.9 copy-start.4
  506.6 3.5 copy-start.8
  513.5 9.9 %collective-permute-start.9 = (bf16[1280,128]{1,0:T(8,128)(2,1)S(1)}, bf16[1280,128]{1,0:T(8,128)(2,1)S(1)}, u32[]{:S(2)}, u32[]{:S(2)}) collective-permute-start(bf16[1280,128]{1,0:T(8,128)(2,1)S(1)} %select_convert_fusion), channel_id=1, source_target_pairs={{0,4},{4,0},{8,12},{12,8},{16,20},{20,16},{24,28},{28,24},{1,5},{5... | collective-permute-start | bytes 983048 | tf_op jit(solution)/shard_map/ppermute | solution.py:11
Sparse Core Ops, SparseCore 0:
  52.9 80.3 all-gather.9
  201.1 44.1 all-gather.11
  297.7 25.4 all-gather.13
  341.6 83.6 all-reduce.1
  488.5 16.6 all-gather.7
